TPU v7x, 32 devices: a whole 2x2x4 slice. The times are simulated.
32 devices in a mesh: parts: 2 (over y), tensor: 4 (over z), dp: 4 (over x, core).
Axes of the slice: x: 2, y: 2, z: 4, core: 2. Of those that a mesh axis runs over, the one named last changes fastest.
Arguments:
- inputs: bfloat16 [4096, 8192], P(('parts', 'dp'), 'tensor'), parts along dimension 0, may hold values from -6 to 6
- cotangent: bfloat16 [4096, 8192], P(('parts', 'dp'), 'tensor'), parts along dimension 0, may hold values from -6 to 6
- weight: bfloat16 [8192, 8192], P(None, 'tensor'), may hold values from -0.0625 to 0.0625
- down_weight_maps: bfloat16 [8192, 2048], P('tensor', 'parts'), parts along dimension 1, may hold values from -0.0625 to 0.0625
- up_weight_maps: bfloat16 [2048, 8192], P('parts', 'tensor'), parts along dimension 0, may hold values from -0.75 to 0.75
- counts: int32 [8, 16], P('parts'), parts along dimension 0, may hold values from 0 to 256, as said below
- ranks: int32 [32], P('parts'), parts along dimension 0, may hold values from 8 to 64, as said below
- owners: int32 [32], P('parts'), parts along dimension 0, may hold values from 0 to 3
Outputs:
- projected: bfloat16 [4096, 8192], P(('parts', 'dp'), 'tensor'), parts along dimension 0
- input_grad: bfloat16 [4096, 8192], P(('parts', 'dp'), 'tensor'), parts along dimension 0
- grad_a: float32 [8, 8192, 1024], P(('parts', 'dp'), 'tensor'), parts along dimension 0
- grad_b: float32 [8, 1024, 8192], P(('parts', 'dp'), None, 'tensor'), parts along dimension 0
There are 2 independent parts, one for each index of `parts`. A program takes and returns all parts, laid end to end along the dimension named above; an argument that names none is the same for every part. Nothing has to cross between parts.
Inputs may be any that keep to these rules, and one draw needn't show every extreme that they name: `counts`: each row sums to at most 512, one row to exactly 512, and all rows together to exactly 1024; some entry is exactly 256. `ranks`: each rank is 64 divided by 1, 2, 4 or 8; some trial has 64 and some 64 // 8.
All inputs are finite; a program needn't handle non-finite values.
Results may differ from a plain program's by a relative error of at most 0.0034.
Values may be sent and summed in bfloat16 or wider, within the bound.
A program may use at most 256 MiB of HBM per device.

v0:
```python
import jax
import jax.numpy as jnp
from jax import lax
from jax.sharding import PartitionSpec as P

LARGEST_RANK = 64
TRIALS = 16
adapter_alpha = 16.0


def local(inputs, cotangent, weight, down_weight_maps, up_weight_maps, counts, ranks, owners):
    slot_count, feature_local = inputs.shape
    group_count = counts.shape[0]
    adapter_rank_width = down_weight_maps.shape[1]
    column = jnp.arange(adapter_rank_width, dtype=jnp.int32)
    col_trial = column // LARGEST_RANK
    column_slot = column % LARGEST_RANK
    trial_ids = jnp.arange(TRIALS, dtype=jnp.int32)
    matches = col_trial[:, None] == trial_ids[None, :]
    rank_per_column = jnp.sum(jnp.where(matches, ranks[None, :], 0), axis=1)
    owner_col = jnp.sum(jnp.where(matches, owners[None, :], 0), axis=1)
    scale_per_column = jnp.where(
        column_slot < rank_per_column, adapter_alpha / rank_per_column.astype(jnp.float32), 0.0
    )
    trial_rows = jnp.sum(counts, axis=0)
    per_trial = 1.0 / jnp.maximum(trial_rows, 1).astype(jnp.float32)
    inverse_col = jnp.sum(jnp.where(matches, per_trial[None, :], 0.0), axis=1)
    cumulative = jnp.cumsum(counts, axis=1)
    group_ids = jnp.arange(group_count, dtype=jnp.int32)
    my_group = lax.axis_index("dp")
    contract_trailing = (((1,), (1,)), ((), ()))
    contract_first = (((0,), (0,)), ((), ()))
    positions = jnp.arange(slot_count, dtype=jnp.int32)
    my_bounds = jnp.sum(jnp.where((group_ids == my_group)[:, None], cumulative, 0), axis=0)
    row_trial = jnp.sum((positions[:, None] >= my_bounds[None, :]).astype(jnp.int32), axis=1)
    is_live = row_trial < TRIALS
    coef = jnp.where(row_trial[:, None] == col_trial[None, :], scale_per_column[None, :], 0.0)
    frozen_output = jnp.dot(
        lax.all_gather(inputs, "tensor", axis=1, tiled=True),
        weight,
        preferred_element_type=jnp.float32,
    )
    down_projected_sum = lax.psum(
        jnp.dot(inputs, down_weight_maps, preferred_element_type=jnp.float32), "tensor"
    )
    scaled_down_projected = (coef * down_projected_sum).astype(jnp.bfloat16)
    merged_output = frozen_output + jnp.dot(
        scaled_down_projected, up_weight_maps, preferred_element_type=jnp.float32
    )
    result = jnp.where(is_live[:, None], merged_output, 0.0).astype(jnp.bfloat16)
    back_part = lax.dot_general(
        cotangent, up_weight_maps, contract_trailing, preferred_element_type=jnp.float32
    )
    back_sum = lax.psum(back_part, "tensor")
    scaled_up_projected = (coef * back_sum).astype(jnp.bfloat16)
    frozen_back = lax.dot_general(
        cotangent, weight, contract_trailing, preferred_element_type=jnp.float32
    )
    frozen_share = lax.psum_scatter(frozen_back, "tensor", scatter_dimension=1, tiled=True)
    adapter_in = lax.dot_general(
        scaled_up_projected, down_weight_maps, contract_trailing, preferred_element_type=jnp.float32
    )
    gradient = jnp.where(is_live[:, None], frozen_share + adapter_in, 0.0).astype(jnp.bfloat16)
    term_a = (
        lax.dot_general(
            inputs, scaled_up_projected, contract_first, preferred_element_type=jnp.float32
        )
        * inverse_col[None, :]
    )
    term_b = (
        lax.dot_general(
            scaled_down_projected, cotangent, contract_first, preferred_element_type=jnp.float32
        )
        * inverse_col[:, None]
    )
    projected, input_grad, term_a, term_b = (result, gradient, term_a, term_b)
    full_a, full_b = lax.psum((term_a, term_b), "dp")
    owned_mine = (owner_col == my_group).astype(jnp.float32)
    grad_a = (full_a * owned_mine[None, :])[None]
    grad_b = (full_b * owned_mine[:, None])[None]
    return (projected, input_grad, grad_a, grad_b)


def solution(mesh):
    return jax.shard_map(
        local,
        mesh=mesh,
        in_specs=(
            P(("parts", "dp"), "tensor"),
            P(("parts", "dp"), "tensor"),
            P(None, "tensor"),
            P("tensor", "parts"),
            P("parts", "tensor"),
            P("parts", None),
            P("parts"),
            P("parts"),
        ),
        out_specs=(
            P(("parts", "dp"), "tensor"),
            P(("parts", "dp"), "tensor"),
            P(("parts", "dp"), "tensor", None),
            P(("parts", "dp"), None, "tensor"),
        ),
        check_vma=False,
    )
```

profile of v0, /device:TPU:0, one launch (start us, length us, event | category | flops | bytes accessed | tf_op | source)
XLA Modules:
  0.0 924.6 jit_solution(6488323135650758244)
XLA Ops:
  7.2 0.0 copy-start
  7.2 0.0 all-reduce.7.cloned.1.call-start
  7.2 0.0 copy-start.7
  7.2 6.6 fusion.15
  13.9 3.7 fusion.17
  17.6 0.0 all-reduce.7.cloned.1.call-update
  17.6 0.0 all-reduce.5.cloned.1.call-start
  17.6 0.6 copy-done.4
  18.2 0.2 reduce_window_sum.11
  18.5 0.1 select_reduce_fusion.3
  18.5 0.1 convert_reduce_fusion
  18.6 0.1 select_reduce_fusion.1
  18.8 0.1 select_reduce_fusion
  18.9 156.9 %all-reduce.7.cloned.1.call-done = (f32[512,1024]{1,0:T(8,128)}, f32[512,1024]{1,0:T(8,128)}) async-done(((f32[512,1024]{1,0:T(8,128)}, f32[512,1024]{1,0:T(8,128)}), (f32[512,1024]{1,0:T(8,128)}, f32[512,1024]{1,0:T(8,128)})) %all-reduce.7.cloned.1.call-update) | async-done | bytes 4194320 | tf_op jit(solution)/shard_map/psum | solution.py:43
  175.8 8.2 multiply_bitcast_fusion.2
  184.0 5.9 convolution_multiply_fusion
  189.9 0.0 all-reduce.5.cloned.1.call-update
  190.0 0.0 all-gather.2.cloned.1.call-start
  190.0 0.7 all-gather.2.cloned.1.call-update
  190.7 0.2 reduce-scatter.2.cloned.1.call-start
  190.9 25.8 %fusion.16 = f32[512,8192]{1,0:T(8,128)} fusion(bf16[512,2048]{1,0:T(8,128)(2,1)S(1)} %copy-done, bf16[8192,2048]{1,0:T(8,128)(2,1)} %param.10), kind=kOutput, calls=%fused_computation.36 | convolution fusion | flops 17179869184 | bytes 52428800 | tf_op jit(solution)/shard_map/dot_general | solution.py:56
  216.7 0.0 reduce-scatter.2.cloned.1.call-update
  216.8 1.6 copy-done.3
  218.4 6.5 fusion.13
  224.9 253.1 %all-reduce.5.cloned.1.call-done = (f32[2048,1024]{0,1:T(8,128)}, f32[1024,2048]{1,0:T(8,128)}) async-done(((f32[2048,1024]{0,1:T(8,128)}, f32[1024,2048]{1,0:T(8,128)}), (f32[2048,1024]{0,1:T(8,128)}, f32[1024,2048]{1,0:T(8,128)})) %all-reduce.5.cloned.1.call-update) | async-done | bytes 16777232 | tf_op jit(solution)/shard_map/psum | solution.py:77
  478.0 7.4 multiply_bitcast_fusion.1
  485.3 9.7 %copy.13 = f32[1,2048,1024]{2,1,0:T(8,128)} copy(f32[1,2048,1024]{1,2,0:T(8,128)} %multiply_bitcast_fusion.1) | data formatting | bytes 16777216
  495.1 7.4 multiply_bitcast_fusion
  502.5 126.8 %all-gather.2.cloned.1.call-done = bf16[512,8192]{1,0:T(8,128)(2,1)} async-done(((bf16[512,2048]{1,0:T(8,128)(2,1)}), bf16[512,8192]{1,0:T(8,128)(2,1)}) %all-gather.2.cloned.1.call-update) | async-done | bytes 8388624 | tf_op jit(solution)/shard_map/all_gather | solution.py:39
  629.3 24.9 %select_convert_fusion.1 = bf16[512,2048]{1,0:T(8,128)(2,1)} fusion(f32[512,2048]{1,0:T(8,128)} %fusion.13, bf16[512,8192]{1,0:T(8,128)(2,1)} %all-gather.2.cloned.1.call-done, bf16[8192,2048]{1,0:T(8,128)(2,1)} %param.10, pred[512]{0:T(512)(128)(4,1)S(1)} %broadcast_compare_fusion), kind=kOutput, calls=%fused_computation.5 | convolution fusion | flops 17183014912 | bytes 48235008 | tf_op jit(solution)/shard_map/dot_general | solution.py:38
  654.2 255.9 %reduce-scatter.2.cloned.1.call-done = f32[512,2048]{1,0:T(8,128)} async-done(((f32[512,8192]{1,0:T(8,128)}), f32[512,2048]{1,0:T(8,128)}) %reduce-scatter.2.cloned.1.call-update) | async-done | bytes 4194320 | tf_op jit(solution)/shard_map/reduce_scatter | solution.py:59
  910.1 7.9 select_convert_fusion
  (19 shorter events, 0.1 us)
Async XLA Ops:
  7.2 6.7 copy-start
  7.2 168.6 %all-reduce.7.cloned.1.call-start = ((), (), s32[]{:S(2)}) async-start(), calls=%async_computation.4 | async-start | bytes 8388608 | tf_op jit(solution)/shard_map/psum | solution.py:43
  7.2 6.6 copy-start.7
  17.5 0.7 copy-start.4
  17.6 1.2 copy-start.5
  17.6 1.2 copy-start.6
  17.6 460.4 %all-reduce.5.cloned.1.call-start = ((), (), s32[]{:S(2)}) async-start(), calls=%async_computation.3 | async-start | bytes 33554432 | tf_op jit(solution)/shard_map/psum | solution.py:77
  175.8 8.3 copy-start.2
  190.0 439.3 %all-gather.2.cloned.1.call-start = ((), (), s32[]{:S(2)}) async-start(), calls=%async_computation.1 | async-start | bytes 10485760 | tf_op jit(solution)/shard_map/all_gather | solution.py:39
  190.7 719.4 %reduce-scatter.2.cloned.1.call-start = ((), (), s32[]{:S(2)}) async-start(), calls=%async_computation.2 | async-start | bytes 20971520 | tf_op jit(solution)/shard_map/reduce_scatter | solution.py:59
  216.7 1.7 copy-start.3
  910.1 7.9 copy-start.1
Sparse Core Ops, SparseCore 0:
  17.7 158.0 all-reduce.6
  190.1 287.8 all-reduce.4
  479.6 149.6 all-gather.1
  631.6 278.4 reduce-scatter.1
where the time goes:
time: 925 us
  waiting for transfers between devices  793 us (86%)
  matrix products  89.6 us (10%)
  other arithmetic  15.4 us (2%)
  between operations  13.9 us (2%)
  local copies, waits for them, and re-layouts  12 us (1%)
    reduce_scatter x1, waiting for transfers between devices, local(): lax.psum_scatter(frozen_back, 'tensor', scatter_dimension=1, tiled=True)  256 us
    psum x1, waiting for transfers between devices, local(): full_a, full_b = lax.psum((term_a, term_b), 'dp')  253 us
    psum x1, waiting for transfers between devices, local(): lax.psum(jnp.dot(inputs, down_weight_maps, preferred_element_type=jnp.flo...  157 us
    all_gather x1, waiting for transfers between devices, local(): lax.all_gather(inputs, 'tensor', axis=1, tiled=True)  127 us
    dot_general x1, matrix products, local(): lax.dot_general(cotangent, weight, contract_trailing, preferred_element_t...  25.8 us
    dot_general x1, matrix products, local(): jnp.dot(lax.all_gather(inputs, 'tensor', axis=1, tiled=True), weight, pre...  24.9 us
  transfers between devices with their start and end apart: 4, of which 4 were waited for; matrix products, arithmetic and copies ran while one was open for 9% of the time, Pallas kernels for 0%

commit v1 on v0

--- a/solution.py
+++ b/solution.py
@@ -2,6 +2,7 @@
 import jax.numpy as jnp
 from jax import lax
 from jax.sharding import PartitionSpec as P
+from jax.lax import axis_index, axis_size, ppermute
 
 LARGEST_RANK = 64
 TRIALS = 16
@@ -35,11 +36,35 @@
     row_trial = jnp.sum((positions[:, None] >= my_bounds[None, :]).astype(jnp.int32), axis=1)
     is_live = row_trial < TRIALS
     coef = jnp.where(row_trial[:, None] == col_trial[None, :], scale_per_column[None, :], 0.0)
-    frozen_output = jnp.dot(
-        lax.all_gather(inputs, "tensor", axis=1, tiled=True),
-        weight,
-        preferred_element_type=jnp.float32,
-    )
+
+    def clear_rates_up(xs):
+        comm_axis = "tensor"
+        t1 = axis_size(comm_axis)
+        frame_out = axis_index(comm_axis)
+        y1, d_next, clean = (t1, frame_out, xs.shape[1])
+        runs = [dev_i * y1 if src_i == 1 else dev_i for src_i, dev_i in enumerate(xs.shape)]
+        newest = jnp.zeros(runs, xs.dtype)
+        latest = lax.dynamic_update_slice_in_dim(newest, xs, d_next * clean, axis=1)
+        formed = current_block = xs
+        for s in range(1, y1 // 2 + 1):
+            current_value = range(y1)
+            arr_now = map(lambda src_i: (src_i, (src_i + 1) % y1), current_value)
+            z_new = list(arr_now)
+            formed = ppermute(formed, comm_axis, z_new)
+            latest = lax.dynamic_update_slice_in_dim(
+                latest, formed, (d_next - s) % y1 * clean, axis=1
+            )
+            if 2 * s < y1:
+                view_out = range(y1)
+                part_next = map(lambda src_i: (src_i, (src_i - 1) % y1), view_out)
+                spare = list(part_next)
+                current_block = ppermute(current_block, comm_axis, spare)
+                latest = lax.dynamic_update_slice_in_dim(
+                    latest, current_block, (d_next + s) % y1 * clean, axis=1
+                )
+        return latest
+
+    frozen_output = jnp.dot(clear_rates_up(inputs), weight, preferred_element_type=jnp.float32)
     down_projected_sum = lax.psum(
         jnp.dot(inputs, down_weight_maps, preferred_element_type=jnp.float32), "tensor"
     )

time: 925 us -> 776 us (0.84)
  waiting for transfers between devices: 793 us -> 641 us
    psum x1, waiting for transfers between devices: 253 us -> 95 us  [local(): full_a, full_b = lax.psum((term_a, term_b), 'dp')]
    ppermute x0 -> x3, waiting for transfers between devices: none -> 130 us  [the longest x2 91.5 us: clear_rates_up(): formed = ppermute(formed, comm_axis, z_new)]
    all_gather x1 -> x0, waiting for transfers between devices: 127 us -> none  [local(): lax.all_gather(inputs, 'tensor', axis=1, tiled=True)]
  transfers between devices with their start and end apart: 4 -> 6, of which waited for: 4 -> 6; matrix products, arithmetic and copies ran while one was open for 9% -> 11% of each run, Pallas kernels for 0% -> 0%
where the time goes in v1:
time: 776 us; the launch traced here: 775 us
  waiting for transfers between devices  641 us (83%)
  matrix products  82.5 us (11%)
  local copies, waits for them, and re-layouts  18.6 us (2%)
  other arithmetic  15.4 us (2%)
  between operations  13.9 us (2%)
    reduce_scatter x1, waiting for transfers between devices, local(): lax.psum_scatter(frozen_back, 'tensor', scatter_dimension=1, tiled=True)  258 us
    psum x1, waiting for transfers between devices, local(): lax.psum(jnp.dot(inputs, down_weight_maps, preferred_element_type=jnp.flo...  157 us
    psum x1, waiting for transfers between devices, local(): full_a, full_b = lax.psum((term_a, term_b), 'dp')  95 us
    ppermute x2, waiting for transfers between devices, clear_rates_up(): formed = ppermute(formed, comm_axis, z_new)  91.5 us
    ppermute x1, waiting for transfers between devices, clear_rates_up(): current_block = ppermute(current_block, comm_axis, spare)  38.8 us
    dot_general x1, matrix products, local(): lax.dot_general(cotangent, weight, contract_trailing, preferred_element_t...  25.1 us
    dot_general x1, matrix products, local(): jnp.dot(clear_rates_up(inputs), weight, preferred_element_type=jnp.float32)  22.5 us
  transfers between devices with their start and end apart: 6, of which 6 were waited for; matrix products, arithmetic and copies ran while one was open for 11% of the time, Pallas kernels for 0%

profile of v1, /device:TPU:0, one launch (start us, length us, event | category | flops | bytes accessed | tf_op | source)
XLA Modules:
  0.0 775.3 jit_solution(12353949350664718951)
XLA Ops:
  7.2 6.6 fusion.15
  13.9 3.7 fusion.17
  17.6 0.0 all-reduce.5.cloned.1.call-start
  17.6 0.6 copy-done.5
  18.2 0.2 reduce_window_sum.11
  18.5 0.1 select_reduce_fusion.3
  18.5 0.1 convert_reduce_fusion
  18.6 0.1 select_reduce_fusion.1
  18.8 0.1 select_reduce_fusion
  18.9 156.9 %all-reduce.7.cloned.1.call-done = (f32[512,1024]{1,0:T(8,128)}, f32[512,1024]{1,0:T(8,128)}) async-done(((f32[512,1024]{1,0:T(8,128)}, f32[512,1024]{1,0:T(8,128)}), (f32[512,1024]{1,0:T(8,128)}, f32[512,1024]{1,0:T(8,128)})) %all-reduce.7.cloned.1.call-update) | async-done | bytes 4194320 | tf_op jit(solution)/shard_map/psum | solution.py:68
  175.8 8.2 %multiply_bitcast_fusion.2 = f32[2048,1024]{0,1:T(8,128)} fusion(bf16[512,2048]{1,0:T(8,128)(2,1)} %param.8, f32[1024]{0:T(1024)S(1)} %select_reduce_fusion.1, f32[512,1024]{1,0:T(8,128)} %get-tuple-element.17, f32[1024]{0:T(1024)S(1)} %divide_select_fusion, s32[1024]{0:T(1024)S(1)} %add_select_fusion, s32[512]{0:T(512)S(1)} %convert_reduce_fusion), kind=kOutput, calls=%fused_computation.2 | convolution fusion | flops 2151677952 | bytes 12597248 | tf_op jit(solution)/shard_map/dot_general | solution.py:90
  184.0 5.9 convolution_multiply_fusion
  190.0 0.2 reduce-scatter.2.cloned.1.call-start
  190.2 25.1 %fusion.16 = f32[512,8192]{1,0:T(8,128)} fusion(bf16[512,2048]{1,0:T(8,128)(2,1)S(1)} %copy-done, bf16[8192,2048]{1,0:T(8,128)(2,1)} %param.10), kind=kOutput, calls=%fused_computation.40 | convolution fusion | flops 17179869184 | bytes 52428800 | tf_op jit(solution)/shard_map/dot_general | solution.py:81
  215.3 1.6 copy-done.2
  216.9 3.8 collective-permute-start.1
  220.7 46.6 %collective-permute-done = bf16[512,2048]{1,0:T(8,128)(2,1)} collective-permute-done((bf16[512,2048]{1,0:T(8,128)(2,1)S(1)}, bf16[512,2048]{1,0:T(8,128)(2,1)}, u32[]{:S(2)}, u32[]{:S(2)}) %collective-permute-start) | collective-permute-done | bytes 2097184 | tf_op jit(solution)/shard_map/ppermute | solution.py:53
  267.4 1.0 broadcast_in_dim.103
  268.4 0.3 constant_dynamic-update-slice_fusion.3
  268.6 1.9 constant_dynamic-update-slice_fusion.2
  270.5 38.8 %collective-permute-done.1 = bf16[512,2048]{1,0:T(8,128)(2,1)} collective-permute-done((bf16[512,2048]{1,0:T(8,128)(2,1)S(1)}, bf16[512,2048]{1,0:T(8,128)(2,1)}, u32[]{:S(2)}, u32[]{:S(2)}) %collective-permute-start.1) | collective-permute-done | bytes 2097184 | tf_op jit(solution)/shard_map/ppermute | solution.py:61
  309.3 1.8 constant_dynamic-update-slice_fusion.1
  311.2 44.9 %collective-permute-done.2 = bf16[512,2048]{1,0:T(8,128)(2,1)} collective-permute-done((bf16[512,2048]{1,0:T(8,128)(2,1)}, bf16[512,2048]{1,0:T(8,128)(2,1)}, u32[]{:S(2)}, u32[]{:S(2)}) %collective-permute-start.2) | collective-permute-done | bytes 2097184 | tf_op jit(solution)/shard_map/ppermute | solution.py:53
  356.1 1.9 constant_dynamic-update-slice_fusion
  358.0 2.5 fusion.13
  360.4 22.5 %select_convert_fusion.1 = bf16[512,2048]{1,0:T(8,128)(2,1)} fusion(f32[512,2048]{1,0:T(8,128)S(1)} %fusion.13, bf16[512,8192]{1,0:T(8,128)(2,1)S(1)} %constant_dynamic-update-slice_fusion, bf16[8192,2048]{1,0:T(8,128)(2,1)} %param.10, pred[512]{0:T(512)(128)(4,1)S(1)} %broadcast_compare_fusion), kind=kOutput, calls=%fused_computation.5 | convolution fusion | flops 17183014912 | bytes 48235008 | tf_op jit(solution)/shard_map/dot_general | solution.py:67
  383.0 95.0 %all-reduce.5.cloned.1.call-done = (f32[2048,1024]{0,1:T(8,128)}, f32[1024,2048]{1,0:T(8,128)}) async-done(((f32[2048,1024]{0,1:T(8,128)}, f32[1024,2048]{1,0:T(8,128)}), (f32[2048,1024]{0,1:T(8,128)}, f32[1024,2048]{1,0:T(8,128)})) %all-reduce.5.cloned.1.call-update) | async-done | bytes 16777232 | tf_op jit(solution)/shard_map/psum | solution.py:102
  478.0 7.4 multiply_bitcast_fusion.1
  485.3 9.6 %copy.13 = f32[1,2048,1024]{2,1,0:T(8,128)} copy(f32[1,2048,1024]{1,2,0:T(8,128)} %multiply_bitcast_fusion.1) | data formatting | bytes 16777216
  494.9 7.5 multiply_bitcast_fusion
  502.4 258.4 %reduce-scatter.2.cloned.1.call-done = f32[512,2048]{1,0:T(8,128)} async-done(((f32[512,8192]{1,0:T(8,128)}), f32[512,2048]{1,0:T(8,128)}) %reduce-scatter.2.cloned.1.call-update) | async-done | bytes 4194320 | tf_op jit(solution)/shard_map/reduce_scatter | solution.py:84
  760.8 7.9 %select_convert_fusion = bf16[512,2048]{1,0:T(8,128)(2,1)} fusion(f32[512,2048]{1,0:T(8,128)} %reduce-scatter.2.cloned.1.call-done, bf16[2048,1024]{1,0:T(8,128)(2,1)} %param.11, pred[512]{0:T(512)(128)(4,1)S(1)} %broadcast_compare_fusion, f32[512,1024]{1,0:T(8,128)} %get-tuple-element.17, f32[1024]{0:T(1024)S(1)} %divide_select_fusion, ...), kind=kOutput, calls=%fused_computation.4 | convolution fusion | flops 2152726528 | bytes 12593664 | tf_op jit(solution)/shard_map/dot_general | solution.py:85
  (31 shorter events, 0.2 us)
Async XLA Ops:
  7.2 6.7 copy-start
  7.2 168.6 %all-reduce.7.cloned.1.call-start = ((), (), s32[]{:S(2)}) async-start(), calls=%async_computation.3 | async-start | bytes 8388608 | tf_op jit(solution)/shard_map/psum | solution.py:68
  7.2 6.6 copy-start.8
  17.5 0.7 copy-start.5
  17.6 1.2 copy-start.6
  17.6 1.2 copy-start.7
  17.6 460.4 %all-reduce.5.cloned.1.call-start = ((), (), s32[]{:S(2)}) async-start(), calls=%async_computation.2 | async-start | bytes 33554432 | tf_op jit(solution)/shard_map/psum | solution.py:102
  175.8 8.3 %copy-start.3 = (f32[512,1024]{1,0:T(8,128)S(1)}, f32[512,1024]{1,0:T(8,128)}, u32[]{:S(2)}) copy-start(f32[512,1024]{1,0:T(8,128)} %get-tuple-element.16) | copy-start | bytes 6291460
  190.0 570.8 %reduce-scatter.2.cloned.1.call-start = ((), (), s32[]{:S(2)}) async-start(), calls=%async_computation.1 | async-start | bytes 20971520 | tf_op jit(solution)/shard_map/reduce_scatter | solution.py:84
  215.3 1.6 copy-start.2
  216.9 50.4 %collective-permute-start = (bf16[512,2048]{1,0:T(8,128)(2,1)S(1)}, bf16[512,2048]{1,0:T(8,128)(2,1)}, u32[]{:S(2)}, u32[]{:S(2)}) collective-permute-start(bf16[512,2048]{1,0:T(8,128)(2,1)S(1)} %copy-done.2), channel_id=1, source_target_pairs={{0,4},{4,8},{8,12},{12,0},{1,5},{5,9},{9,13},{13,1},{2,6},{6,10},{... | collective-permute-start | bytes 6291464 | tf_op jit(solution)/shard_map/ppermute | solution.py:53
  216.9 92.4 %collective-permute-start.1 = (bf16[512,2048]{1,0:T(8,128)(2,1)S(1)}, bf16[512,2048]{1,0:T(8,128)(2,1)}, u32[]{:S(2)}, u32[]{:S(2)}) collective-permute-start(bf16[512,2048]{1,0:T(8,128)(2,1)S(1)} %copy-done.2), channel_id=1, source_target_pairs={{0,12},{4,0},{8,4},{12,8},{1,13},{5,1},{9,5},{13,9},{2,14},{6,2},{... | collective-permute-start | bytes 6291464 | tf_op jit(solution)/shard_map/ppermute | solution.py:61
  267.3 88.7 %collective-permute-start.2 = (bf16[512,2048]{1,0:T(8,128)(2,1)}, bf16[512,2048]{1,0:T(8,128)(2,1)}, u32[]{:S(2)}, u32[]{:S(2)}) collective-permute-start(bf16[512,2048]{1,0:T(8,128)(2,1)} %collective-permute-done), channel_id=1, source_target_pairs={{0,4},{4,8},{8,12},{12,0},{1,5},{5,9},{9,13},{13,1},{2,6},{6,10},{... | collective-permute-start | bytes 6291464 | tf_op jit(solution)/shard_map/ppermute | solution.py:53
  270.5 87.4 %copy-start.4 = (f32[512,1024]{1,0:T(8,128)S(1)}, f32[512,1024]{1,0:T(8,128)}, u32[]{:S(2)}) copy-start(f32[512,1024]{1,0:T(8,128)} %get-tuple-element.16) | copy-start | bytes 6291460
  270.5 87.4 %copy-start.9 = (bf16[1024,2048]{1,0:T(8,128)(2,1)S(1)}, bf16[1024,2048]{1,0:T(8,128)(2,1)}, u32[]{:S(2)}) copy-start(bf16[1024,2048]{1,0:T(8,128)(2,1)} %param.12) | copy-start | bytes 12582916
  760.8 7.9 %copy-start.1 = (bf16[512,2048]{1,0:T(8,128)(2,1)S(1)}, bf16[512,2048]{1,0:T(8,128)(2,1)}, u32[]{:S(2)}) copy-start(bf16[512,2048]{1,0:T(8,128)(2,1)} %param.9) | copy-start | bytes 6291460
Sparse Core Ops, SparseCore 0:
  17.7 158.0 all-reduce.6
  190.1 287.8 all-reduce.4
  480.4 280.3 reduce-scatter.1
